TPU v7x, 256 devices: a whole 4x4x8 slice. The times are simulated.
256 devices in a mesh: dp: 32 (over z_lo, x, core), group: 8 (over y, z_hi).
Axes of the slice: x: 4, y: 4, z: 8 (z_hi: 2, z_lo: 4; z = z_hi * 4 + z_lo), core: 2. Of those that a mesh axis runs over, the one named last changes fastest.
Arguments:
- tokens: bfloat16 [32768, 7168], P('dp', 'group'), may hold values from -6 to 6
- proj_in: bfloat16 [32, 1024, 2, 7168], P(None, 'dp', None, 'group'), may hold values from -0.0625 to 0.0625
- proj_out: bfloat16 [32, 1024, 7168], P(None, 'dp', 'group'), may hold values from -0.1875 to 0.1875
- expert_list: int32 [32, 2], replicated, may hold values from 0 to 31, as said below
- block_pattern: int32 [32, 2, 8], replicated, may hold values from 0 to 1, as said below
- route_weight: float32 [32768, 2], P('dp'), may hold values from 0.1 to 1
Outputs:
- mixed: bfloat16 [32768, 7168], P('dp', 'group')
Inputs may be any that keep to these rules, and one draw needn't show every extreme that they name: `expert_list`: each row names 2 different experts of the window. `block_pattern`: 1 where the list slot's expert acts on that block of 128 tokens, else 0; the share of ones differs from token group to token group, and in every draw some token group has every block of every slot set.
All inputs are finite; a program needn't handle non-finite values.
Results may differ from a plain program's by a relative error of at most 0.025.
Values may be sent and summed in bfloat16 or wider, within the bound.
A program may use at most 128 MiB of HBM per device.

v0:
```python
import jax
import jax.numpy as jnp
from jax import lax
from jax.sharding import PartitionSpec as P


def on_device(tokens, proj_in, proj_out, expert_list, block_pattern, route_weight):
    group_size = lax.axis_size("group")
    dp_index = lax.axis_index("dp")
    group_index = lax.axis_index("group")
    row_count = tokens.shape[0]
    slots = expert_list.shape[1]
    block_rows = row_count // block_pattern.shape[2]
    share_rows = row_count // group_size
    width_here = tokens.shape[1]
    requested = expert_list.T.reshape(-1)
    send_in = jnp.take(proj_in, requested, axis=0).reshape(slots, -1, 2, width_here)
    send_out = jnp.take(proj_out, requested, axis=0).reshape(slots, -1, width_here)
    own_pattern = lax.dynamic_index_in_dim(block_pattern, dp_index, 0, keepdims=False)
    block_mask = jnp.repeat(own_pattern, block_rows, axis=1).astype(jnp.float32)
    token_scale = route_weight.T * block_mask
    weight_in = lax.all_to_all(send_in, "dp", split_axis=1, concat_axis=1, tiled=True)
    weight_out = lax.all_to_all(send_out, "dp", split_axis=1, concat_axis=1, tiled=True)
    partial_here = jnp.einsum(
        "td,kfcd->ktcf", tokens, weight_in, preferred_element_type=jnp.float32
    )
    shares = lax.psum_scatter(
        partial_here.astype(jnp.bfloat16), "group", scatter_dimension=1, tiled=True
    ).astype(jnp.float32)
    own_scale = lax.dynamic_slice_in_dim(token_scale, group_index * share_rows, share_rows, 1)
    hidden = (own_scale[:, :, None] * jax.nn.silu(shares[:, :, 0]) * shares[:, :, 1]).astype(
        jnp.bfloat16
    )
    combined = jnp.einsum(
        "ktf,kfd->td",
        lax.all_gather(hidden, "group", axis=1, tiled=True),
        weight_out,
        preferred_element_type=jnp.float32,
    )
    return combined.astype(jnp.bfloat16)


def solution(mesh):
    return jax.shard_map(
        on_device,
        mesh=mesh,
        in_specs=(
            P("dp", "group"),
            P(None, "dp", None, "group"),
            P(None, "dp", "group"),
            P(),
            P(),
            P("dp", None),
        ),
        out_specs=P("dp", "group"),
        check_vma=False,
    )
```

profile of v0, /device:TPU:24, one launch (start us, length us, event | category | flops | bytes accessed | tf_op | source)
XLA Modules:
  0.0 619.6 jit_solution(2263816970232695262)
XLA Ops:
  6.5 0.0 copy-start
  6.5 0.0 reduce-scatter.4.cloned.1.call-start
  6.5 0.8 compare_and_fusion
  7.4 0.1 broadcast_in_dim.29
  7.4 0.1 broadcast_in_dim.30
  7.5 0.8 reshape.51
  8.3 19.4 %gather_fusion = bf16[64,32,2,896]{3,2,1,0:T(2,128)(2,1)} fusion(bf16[32,32,2,896]{3,2,1,0:T(2,128)(2,1)} %param.7, s32[1024]{0:T(1024)S(1)} %pad_clamp_fusion), kind=kCustom, calls=%fused_computation | custom fusion | bytes 14680320 | tf_op jit(solution)/shard_map/jit(_take)/gather | solution.py:17
  27.8 4.2 copy.22
  32.0 3.8 bitcast_select_fusion
  35.8 13.0 %copy.23 = bf16[2,1024,2,896]{3,2,0,1:T(2,128)(2,1)S(1)} copy(bf16[2,1024,2,896]{3,1,0,2:T(8,128)(2,1)} %bitcast_select_fusion) | data formatting | bytes 14680064 | tf_op jit(solution)/shard_map/jit(_take)/select_n | solution.py:17
  48.8 169.6 %all_to_all.10 = bf16[2,1024,2,896]{3,2,0,1:T(2,128)(2,1)S(1)} all-to-all(bf16[2,1024,2,896]{3,2,0,1:T(2,128)(2,1)S(1)} %copy.23), channel_id=1, replica_groups=mesh['dp'=32,'group'=8] {'dp'}, dimensions={1} | all-to-all | bytes 14680064 | tf_op jit(solution)/shard_map/all_to_all | solution.py:22
  218.5 0.0 copy-done
  218.5 11.0 %convert_bitcast_fusion = bf16[2,1024,2,1024]{1,3,2,0:T(8,128)(2,1)} fusion(bf16[2,1024,2,896]{3,2,0,1:T(2,128)(2,1)S(1)} %all_to_all.10, bf16[1024,896]{1,0:T(8,128)(2,1)S(1)} %copy-done), kind=kOutput, calls=%fused_computation.2 | convolution fusion | flops 7520387072 | bytes 17563648 | tf_op jit(solution)/shard_map/td,kfcd->ktcf/dot_general | solution.py:24
  229.5 21.5 %copy.29 = bf16[2,1024,2,1024]{3,2,0,1:T(2,128)(2,1)} copy(bf16[2,1024,2,1024]{1,3,2,0:T(8,128)(2,1)} %convert_bitcast_fusion) | data formatting | bytes 16777216
  250.9 14.4 %reshape.70 = bf16[1024,4096]{1,0:T(8,128)(2,1)} reshape(bf16[1024,2,2,1024]{3,2,1,0:T(2,128)(2,1)} %bitcast.39) | data formatting | bytes 16777216
  265.4 0.0 copy-start.3
  265.4 0.0 copy-start.2
  265.4 0.0 reduce-scatter.4.cloned.1.call-update
  265.4 0.2 all-gather.2.cloned.1.call-start
  265.6 0.4 copy-done.3
  266.1 0.2 convert_reduce_fusion
  266.2 0.1 broadcast_bitcast_fusion
  266.3 0.6 copy-done.2
  266.9 2.8 gather_fusion.1
  269.6 0.7 dynamic-slice_multiply_fusion
  270.3 180.5 %reduce-scatter.4.cloned.1.call-done = bf16[128,4096]{1,0:T(8,128)(2,1)} async-done(((bf16[1024,4096]{1,0:T(8,128)(2,1)}), bf16[128,4096]{1,0:T(8,128)(2,1)}) %reduce-scatter.4.cloned.1.call-update) | async-done | bytes 1048592
  450.8 1.8 reshape.71
  452.6 0.4 copy_convert_fusion
  453.0 1.1 fusion.10
  454.1 0.0 all-gather.2.cloned.1.call-update
  454.2 2.4 bitcast_select_fusion.1
  456.5 3.8 copy.26
  460.3 143.3 %all_to_all.11 = bf16[2,1024,896]{2,0,1:T(2,128)(2,1)} all-to-all(bf16[2,1024,896]{2,0,1:T(2,128)(2,1)S(1)} %copy.26), channel_id=1, replica_groups=mesh['dp'=32,'group'=8] {'dp'}, dimensions={1} | all-to-all | bytes 7340032 | tf_op jit(solution)/shard_map/all_to_all | solution.py:23
  603.6 0.0 all-gather.2.cloned.1.call-done
  603.6 0.0 copy-start.1
  603.6 9.2 %bitcast_convert_fusion = bf16[1024,896]{1,0:T(8,128)(2,1)} fusion(bf16[2,1024,1024]{2,1,0:T(8,128)(2,1)} %all-gather.2.cloned.1.call-done, bf16[2,1024,896]{2,0,1:T(2,128)(2,1)} %all_to_all.11), kind=kOutput, calls=%fused_computation.6 | convolution fusion | flops 3759013888 | bytes 9699328 | tf_op jit(solution)/shard_map/ktf,kfd->td/dot_general | solution.py:34
  612.8 0.0 copy-done.1
  (3 shorter events, 0.0 us)
Async XLA Ops:
  6.5 211.9 %copy-start = (bf16[1024,896]{1,0:T(8,128)(2,1)S(1)}, bf16[1024,896]{1,0:T(8,128)(2,1)}, u32[]{:S(2)}) copy-start(bf16[1024,896]{1,0:T(8,128)(2,1)} %param.6) | copy-start | bytes 5505028
  6.5 444.3 %reduce-scatter.4.cloned.1.call-start = ((), (), s32[]{:S(2)}) async-start(), calls=%async_computation.4 | async-start | bytes 9437184
  265.4 0.7 copy-start.3
  265.4 1.5 copy-start.2
  265.4 338.2 %all-gather.2.cloned.1.call-start = ((), (), s32[]{:S(2)}) async-start(), calls=%async_computation.3 | async-start | bytes 4718592 | tf_op jit(solution)/shard_map/all_gather | solution.py:36
  603.6 9.2 %copy-start.1 = (bf16[1024,896]{1,0:T(8,128)(2,1)S(1)}, bf16[1024,896]{1,0:T(8,128)(2,1)}, u32[]{:S(2)}) copy-start(bf16[1024,896]{1,0:T(8,128)(2,1)} %param.6) | copy-start | bytes 5505028
Sparse Core Ops, SparseCore 0:
  265.5 185.2 reduce-scatter.3
  454.3 135.2 all-gather.1
where the time goes:
time: 623 us; the launch traced here: 620 us
  blocking collectives  313 us (50%)
  waiting for transfers between devices  180 us (29%)
  local copies, waits for them, and re-layouts  83 us (13%)
  matrix products  20.1 us (3%)
  between operations  13.5 us (2%)
  other arithmetic  9.39 us (2%)
    unnamed x3, waiting for transfers between devices  180 us
    all_to_all x1, blocking collectives, on_device(): lax.all_to_all(send_in, 'dp', split_axis=1, concat_axis=1, tiled=True)  170 us
    all_to_all x1, blocking collectives, on_device(): lax.all_to_all(send_out, 'dp', split_axis=1, concat_axis=1, tiled=True)  143 us
    unnamed x13, local copies, waits for them, and re-layouts  38.8 us
    gather x2, local copies, waits for them, and re-layouts, on_device(): jnp.take(proj_in, requested, axis=0).reshape(slots, -1, 2, width_here)  23.7 us
    select_n x1, local copies, waits for them, and re-layouts, on_device(): jnp.take(proj_in, requested, axis=0).reshape(slots, -1, 2, width_here)  13 us
  transfers between devices with their start and end apart: 2, of which 1 were waited for; matrix products, arithmetic and copies ran while one was open for 2% of the time, Pallas kernels for 0%

commit v1 on v0

v1 whole, which is shorter than its diff:
```python
import jax
import jax.numpy as jnp
from jax import lax
from jax.sharding import PartitionSpec as P


def on_device(tokens, proj_in, proj_out, expert_list, block_pattern, route_weight):
    group_size = lax.axis_size("group")
    n_dp = lax.axis_size("dp")
    dp_index = lax.axis_index("dp")
    row_count, width_here = tokens.shape
    slots = expert_list.shape[1]
    ff_here = proj_in.shape[1]
    block_rows = row_count // block_pattern.shape[2]

    own_pattern = lax.dynamic_index_in_dim(block_pattern, dp_index, 0, keepdims=False)
    block_mask = jnp.repeat(own_pattern, block_rows, axis=1).astype(jnp.float32)
    token_scale = route_weight.T * block_mask

    send_in = jnp.take(proj_in, expert_list, axis=0).transpose(0, 1, 3, 2, 4)
    send_out = jnp.take(proj_out, expert_list, axis=0)

    gathered = []
    weights_out = []
    pending = tokens
    for slot in range(slots):
        pending, piece = lax.optimization_barrier((pending, send_in[:, slot]))
        weight_in = lax.all_to_all(piece, "dp", 0, 0, tiled=True).reshape(-1, width_here)
        partial_here = jnp.dot(weight_in, tokens.T, preferred_element_type=jnp.float32)
        partial_here = partial_here.astype(jnp.bfloat16)
        shares = lax.psum_scatter(partial_here, "group", scatter_dimension=0, tiled=True)
        gathered.append(shares)
        pending = partial_here
    for slot in range(slots):
        pending, piece = lax.optimization_barrier((pending, send_out[:, slot]))
        weight_out = lax.all_to_all(piece, "dp", 0, 0, tiled=True)
        weights_out.append(weight_out.reshape(-1, width_here))
        pending = weight_out

    combined = None
    for slot in range(slots):
        shares = gathered[slot].astype(jnp.float32).reshape(n_dp // group_size, 2, ff_here, row_count)
        hidden = (token_scale[slot] * jax.nn.silu(shares[:, 0]) * shares[:, 1]).astype(jnp.bfloat16)
        hidden = lax.all_gather(hidden.reshape(-1, row_count), "group", axis=0, tiled=True)
        term = lax.dot_general(
            hidden, weights_out[slot], (((0,), (0,)), ((), ())), preferred_element_type=jnp.float32
        )
        combined = term if combined is None else combined + term
    return combined.astype(jnp.bfloat16)


def solution(mesh):
    return jax.shard_map(
        on_device,
        mesh=mesh,
        in_specs=(
            P("dp", "group"),
            P(None, "dp", None, "group"),
            P(None, "dp", "group"),
            P(),
            P(),
            P("dp", None),
        ),
        out_specs=P("dp", "group"),
        check_vma=False,
    )
```

time: 623 us -> 598 us (0.960)
  waiting for transfers between devices: 180 us -> 259 us
  blocking collectives: 313 us -> 236 us
  local copies, waits for them, and re-layouts: 83 us -> 40.9 us
  starting transfers between devices: 0.22 us -> 9.65 us
    unnamed x3 -> x4, waiting for transfers between devices: 180 us -> 0.07 us
    all_gather x1 -> x2, waiting for transfers between devices: 0.01 us -> 144 us  [on_device(): lax.all_gather(hidden.reshape(-1, row_count), 'group', axis=0, tiled=True)]
    reduce_scatter x0 -> x2, waiting for transfers between devices: none -> 114 us  [on_device(): lax.psum_scatter(partial_here, 'group', scatter_dimension=0, tiled=True)]
    all_to_all x2, blocking collectives: 313 us -> 236 us  [on_device(): lax.all_to_all(piece, 'dp', 0, 0, tiled=True).reshape(-1, width_here)]
    unnamed x13 -> x11, local copies, waits for them, and re-layouts: 38.8 us -> 1.51 us
    select_n x2 -> x1, local copies, waits for them, and re-layouts: 16.7 us -> 0.09 us  [on_device(): send_in = jnp.take(proj_in, expert_list, axis=0).transpose(0, 1, 3, 2, 4)]
    all_to_all x0 -> x2, starting transfers between devices: none -> 9.52 us  [on_device(): weight_out = lax.all_to_all(piece, 'dp', 0, 0, tiled=True)]
    squeeze x0 -> x2, local copies, waits for them, and re-layouts: none -> 6.87 us  [the longest x1 4.39 us: on_device(): pending, piece = lax.optimization_barrier((pending, send_out[:, slot]))]
  transfers between devices with their start and end apart: 2 -> 6, of which waited for: 1 -> 4; matrix products, arithmetic and copies ran while one was open for 2% -> 5% of each run, Pallas kernels for 0% -> 0%
where the time goes in v1:
time: 598 us; the launch traced here: 596 us
  waiting for transfers between devices  259 us (43%)
  blocking collectives  236 us (39%)
  local copies, waits for them, and re-layouts  40.9 us (7%)
  matrix products  25.8 us (4%)
  between operations  13.2 us (2%)
  other arithmetic  11.6 us (2%)
  starting transfers between devices  9.65 us (2%)
    all_to_all x2, blocking collectives, on_device(): lax.all_to_all(piece, 'dp', 0, 0, tiled=True).reshape(-1, width_here)  236 us
    all_gather x2, waiting for transfers between devices, on_device(): lax.all_gather(hidden.reshape(-1, row_count), 'group', axis=0, tiled=True)  144 us
    reduce_scatter x2, waiting for transfers between devices, on_device(): lax.psum_scatter(partial_here, 'group', scatter_dimension=0, tiled=True)  114 us
    gather x2, local copies, waits for them, and re-layouts, on_device(): send_in = jnp.take(proj_in, expert_list, axis=0).transpose(0, 1, 3, 2, 4)  27.2 us
    dot_general x2, matrix products, on_device(): lax.dot_general(hidden, weights_out[slot], (((0,), (0,)), ((), ())), pref...  13.3 us
    dot_general x2, matrix products, on_device(): jnp.dot(weight_in, tokens.T, preferred_element_type=jnp.float32)  12.6 us
  transfers between devices with their start and end apart: 6, of which 4 were waited for; matrix products, arithmetic and copies ran while one was open for 5% of the time, Pallas kernels for 0%

profile of v1, /device:TPU:24, one launch (start us, length us, event | category | flops | bytes accessed | tf_op | source)
XLA Modules:
  0.0 596.4 jit_solution(7984410373641122394)
XLA Ops:
  6.5 0.0 copy-start
  6.5 0.0 reduce-scatter.3.cloned.1.call-start
  6.5 0.8 compare_select_fusion
  7.4 0.7 compare_and_fusion
  8.0 0.1 copy.16
  8.1 0.1 reshape.54
  8.2 19.4 %gather_fusion = bf16[64,32,2,896]{3,2,1,0:T(2,128)(2,1)} fusion(bf16[32,32,2,896]{3,2,1,0:T(2,128)(2,1)} %param.7, s32[1024]{0:T(1024)S(1)} %pad_clamp_fusion), kind=kCustom, calls=%fused_computation | custom fusion | bytes 14680320 | tf_op jit(solution)/shard_map/jit(_take)/gather | solution.py:20
  27.7 7.7 %copy.17 = bf16[64,32,2,896]{3,1,2,0:T(8,128)(2,1)} copy(bf16[64,32,2,896]{3,2,1,0:T(2,128)(2,1)} %gather_fusion) | data formatting | bytes 14680064 | tf_op jit(solution)/shard_map/jit(_take)/gather | solution.py:20
  35.4 0.1 copy.15
  35.5 3.9 select_bitcast_fusion
  39.4 2.5 slice_bitcast_fusion
  41.9 91.8 %all_to_all.20 = bf16[32,2,32,896]{3,2,1,0:T(8,128)(2,1)S(1)} all-to-all(bf16[32,2,32,896]{3,2,1,0:T(8,128)(2,1)S(1)} %get-tuple-element.9), channel_id=1, replica_groups=mesh['dp'=32,'group'=8] {'dp'}, dimensions={0} | all-to-all | bytes 7340032 | tf_op jit(solution)/shard_map/all_to_all | solution.py:28
  133.7 0.0 copy-done
  133.7 6.3 %convolution_convert_fusion.1 = bf16[2048,1024]{1,0:T(8,128)(2,1)} fusion(bf16[2048,896]{1,0:T(8,128)(2,1)S(1)} %bitcast.76, bf16[1024,896]{1,0:T(8,128)(2,1)S(1)} %copy-done), kind=kOutput, calls=%fused_computation.4 | convolution fusion | flops 3760193536 | bytes 9699328 | tf_op jit(solution)/shard_map/dot_general | solution.py:29
  140.0 0.0 reduce-scatter.3.cloned.1.call-update
  140.0 0.0 reduce-scatter.5.cloned.1.call-start
  140.1 144.2 %all_to_all.21 = bf16[32,2,32,896]{3,2,1,0:T(8,128)(2,1)S(1)} all-to-all(bf16[32,2,32,896]{3,2,1,0:T(8,128)(2,1)} %get-tuple-element.10), channel_id=1, replica_groups=mesh['dp'=32,'group'=8] {'dp'}, dimensions={0} | all-to-all | bytes 7340032 | tf_op jit(solution)/shard_map/all_to_all | solution.py:28
  284.3 6.3 %convolution_convert_fusion = bf16[2048,1024]{1,0:T(8,128)(2,1)} fusion(bf16[2048,896]{1,0:T(8,128)(2,1)S(1)} %bitcast.77, bf16[1024,896]{1,0:T(8,128)(2,1)S(1)} %copy-done), kind=kOutput, calls=%fused_computation.3 | convolution fusion | flops 3760193536 | bytes 9699328 | tf_op jit(solution)/shard_map/dot_general | solution.py:29
  290.6 0.0 copy-start.2
  290.6 0.0 reduce-scatter.5.cloned.1.call-update
  290.6 0.0 all-gather.3.cloned.1.call-start
  290.7 1.4 copy-done.2
  292.1 0.0 copy-start.4
  292.1 0.0 copy-start.3
  292.1 2.8 gather_fusion.1
  294.9 0.0 copy-done.4
  294.9 0.2 convert_reduce_fusion
  295.1 0.1 broadcast_bitcast_fusion
  295.1 0.0 copy-done.3
  295.2 4.3 broadcast_select_fusion
  299.4 1.1 fusion.11
  300.6 0.9 fusion.5
  301.4 0.0 all-gather.3.cloned.1.call-update
  301.5 4.4 slice_bitcast_fusion.2
  305.9 4.8 all-to-all-start.2
  310.6 0.0 all-gather.5.cloned.1.call-start
  310.7 114.1 %reduce-scatter.5.cloned.1.call-done = bf16[256,1024]{1,0:T(8,128)(2,1)} async-done(((bf16[2048,1024]{1,0:T(8,128)(2,1)}), bf16[256,1024]{1,0:T(8,128)(2,1)}) %reduce-scatter.5.cloned.1.call-update) | async-done | bytes 524304 | tf_op jit(solution)/shard_map/reduce_scatter | solution.py:31
  424.7 1.1 fusion.10
  425.9 0.9 fusion
  426.7 0.0 all-gather.5.cloned.1.call-update
  426.8 0.0 all-to-all-done.2
  426.8 4.8 all-to-all-start.3
  431.6 64.1 %all-gather.3.cloned.1.call-done = bf16[1024,1024]{1,0:T(8,128)(2,1)} async-done(((bf16[128,1024]{1,0:T(8,128)(2,1)}), bf16[1024,1024]{1,0:T(8,128)(2,1)}) %all-gather.3.cloned.1.call-update) | async-done | bytes 2097168 | tf_op jit(solution)/shard_map/all_gather | solution.py:44
  495.6 6.3 %fusion.13 = f32[1024,896]{1,0:T(8,128)} fusion(bf16[1024,1024]{1,0:T(8,128)(2,1)} %all-gather.3.cloned.1.call-done, bf16[1024,896]{1,0:T(8,128)(2,1)} %bitcast.14), kind=kOutput, calls=%fused_computation.36 | convolution fusion | flops 1879048192 | bytes 7602176 | tf_op jit(solution)/shard_map/dot_general | solution.py:45
  501.9 0.8 all-to-all-done.3
  502.7 80.1 %all-gather.5.cloned.1.call-done = bf16[1024,1024]{1,0:T(8,128)(2,1)} async-done(((bf16[128,1024]{1,0:T(8,128)(2,1)}), bf16[1024,1024]{1,0:T(8,128)(2,1)}) %all-gather.5.cloned.1.call-update) | async-done | bytes 2097168 | tf_op jit(solution)/shard_map/all_gather | solution.py:44
  582.9 7.0 %add_convert_fusion = bf16[1024,896]{1,0:T(8,128)(2,1)} fusion(f32[1024,896]{1,0:T(8,128)} %fusion.13, bf16[1024,1024]{1,0:T(8,128)(2,1)} %all-gather.5.cloned.1.call-done, bf16[1024,896]{1,0:T(8,128)(2,1)} %bitcast.21), kind=kOutput, calls=%fused_computation.7 | convolution fusion | flops 1880883200 | bytes 9437184 | tf_op jit(solution)/shard_map/dot_general | solution.py:45
  589.8 0.0 copy-done.1
  (5 shorter events, 0.0 us)
Async XLA Ops:
  6.5 127.2 %copy-start = (bf16[1024,896]{1,0:T(8,128)(2,1)S(1)}, bf16[1024,896]{1,0:T(8,128)(2,1)}, u32[]{:S(2)}) copy-start(bf16[1024,896]{1,0:T(8,128)(2,1)} %param.6) | copy-start | bytes 5505028
  6.5 292.9 %reduce-scatter.3.cloned.1.call-start = ((), (), s32[]{:S(2)}) async-start(), calls=%async_computation.6 | async-start | bytes 4718592 | tf_op jit(solution)/shard_map/reduce_scatter | solution.py:31
  140.0 284.7 %reduce-scatter.5.cloned.1.call-start = ((), (), s32[]{:S(2)}) async-start(), calls=%async_computation.8 | async-start | bytes 4718592 | tf_op jit(solution)/shard_map/reduce_scatter | solution.py:31
  290.6 1.5 copy-start.2
  290.6 205.0 %all-gather.3.cloned.1.call-start = ((), (), s32[]{:S(2)}) async-start(), calls=%async_computation.7 | async-start | bytes 2359296 | tf_op jit(solution)/shard_map/all_gather | solution.py:44
  292.1 2.8 copy-start.4
  292.1 3.0 copy-start.3
  305.9 120.9 %all-to-all-start.2 = ((bf16[32,32,896]{2,1,0:T(8,128)(2,1)}), bf16[32,32,896]{2,1,0:T(8,128)(2,1)}, u32[]{:S(2)}, u32[]{:S(2)}) async-start(bf16[32,32,896]{2,1,0:T(8,128)(2,1)} %get-tuple-element.11), calls=%async_computation.3 | async-start | bytes 3670016 | tf_op jit(solution)/shard_map/all_to_all | solution.py:36
  310.6 272.2 %all-gather.5.cloned.1.call-start = ((), (), s32[]{:S(2)}) async-start(), calls=%async_computation.9 | async-start | bytes 2359296 | tf_op jit(solution)/shard_map/all_gather | solution.py:44
  426.8 76.0 %all-to-all-start.3 = ((bf16[32,32,896]{2,1,0:T(8,128)(2,1)}), bf16[32,32,896]{2,1,0:T(8,128)(2,1)}, u32[]{:S(2)}, u32[]{:S(2)}) async-start(bf16[32,32,896]{2,1,0:T(8,128)(2,1)} %get-tuple-element.12), calls=%async_computation.5 | async-start | bytes 3670016 | tf_op jit(solution)/shard_map/all_to_all | solution.py:36
  582.9 7.0 %copy-start.1 = (bf16[1024,896]{1,0:T(8,128)(2,1)S(1)}, bf16[1024,896]{1,0:T(8,128)(2,1)}, u32[]{:S(2)}) copy-start(bf16[1024,896]{1,0:T(8,128)(2,1)} %param.6) | copy-start | bytes 5505028
Sparse Core Ops, SparseCore 0:
  140.2 141.2 reduce-scatter.2
  290.8 133.9 reduce-scatter.4
  427.4 68.2 all-gather.2
  498.1 84.7 all-gather.4

commit v2 on v1

--- a/solution.py
+++ b/solution.py
@@ -2,6 +2,67 @@
 import jax.numpy as jnp
 from jax import lax
 from jax.sharding import PartitionSpec as P
+
+
+Y_PARTS = 4
+
+
+def _perm(size, fn):
+    return [(j, fn(j)) for j in range(size)]
+
+
+def _y_shift(size, dy):
+    z_parts = size // Y_PARTS
+    return _perm(size, lambda j: ((j // z_parts + dy) % Y_PARTS) * z_parts + j % z_parts)
+
+
+def _z_flip(size):
+    return _perm(size, lambda j: j ^ 1)
+
+
+def group_reduce_scatter(x):
+    size = lax.axis_size("group")
+    j = lax.axis_index("group")
+    y, zh = j // 2, j % 2
+    rows = x.shape[0] // Y_PARTS
+    half = rows // 2
+
+    def block(yy):
+        return lax.dynamic_slice_in_dim(x, (yy % Y_PARTS) * rows, rows, 0)
+
+    far = block(y + 2)
+    up = lax.ppermute(block(y + 1), "group", _y_shift(size, 1))
+    down = lax.ppermute(block(y - 1), "group", _y_shift(size, -1))
+    up_far = lax.ppermute(far[:half], "group", _y_shift(size, 1))
+    down_far = lax.ppermute(far[half:], "group", _y_shift(size, -1))
+    relay_up = lax.ppermute(up_far, "group", _y_shift(size, 1))
+    relay_down = lax.ppermute(down_far, "group", _y_shift(size, -1))
+    f32 = jnp.float32
+    y_sum = (
+        block(y).astype(f32) + up.astype(f32) + down.astype(f32)
+        + jnp.concatenate([relay_up, relay_down], axis=0).astype(f32)
+    )
+    mine = lax.dynamic_slice_in_dim(y_sum, zh * half, half, 0)
+    other = lax.dynamic_slice_in_dim(y_sum, (1 - zh) * half, half, 0)
+    return mine + lax.ppermute(other.astype(jnp.bfloat16), "group", _z_flip(size)).astype(f32)
+
+
+def group_all_gather(h):
+    size = lax.axis_size("group")
+    j = lax.axis_index("group")
+    y, zh = j // 2, j % 2
+    n = h.shape[0]
+    partner = lax.ppermute(h, "group", _z_flip(size))
+    pair = jnp.where(zh == 0, jnp.concatenate([h, partner]), jnp.concatenate([partner, h]))
+    from_down = lax.ppermute(pair, "group", _y_shift(size, 1))
+    from_up = lax.ppermute(pair, "group", _y_shift(size, -1))
+    far_a = lax.ppermute(from_down[:n], "group", _y_shift(size, 1))
+    far_b = lax.ppermute(from_up[n:], "group", _y_shift(size, -1))
+    out = jnp.zeros((Y_PARTS * 2 * n,) + h.shape[1:], h.dtype)
+    for dy, piece in ((0, pair), (-1, from_down), (1, from_up),
+                      (2, jnp.concatenate([far_a, far_b]))):
+        out = lax.dynamic_update_slice_in_dim(out, piece, ((y + dy) % Y_PARTS) * 2 * n, 0)
+    return out
 
 
 def on_device(tokens, proj_in, proj_out, expert_list, block_pattern, route_weight):
@@ -28,7 +89,7 @@
         weight_in = lax.all_to_all(piece, "dp", 0, 0, tiled=True).reshape(-1, width_here)
         partial_here = jnp.dot(weight_in, tokens.T, preferred_element_type=jnp.float32)
         partial_here = partial_here.astype(jnp.bfloat16)
-        shares = lax.psum_scatter(partial_here, "group", scatter_dimension=0, tiled=True)
+        shares = group_reduce_scatter(partial_here)
         gathered.append(shares)
         pending = partial_here
     for slot in range(slots):
@@ -39,9 +100,9 @@
 
     combined = None
     for slot in range(slots):
-        shares = gathered[slot].astype(jnp.float32).reshape(n_dp // group_size, 2, ff_here, row_count)
+        shares = gathered[slot].reshape(n_dp // group_size, 2, ff_here, row_count)
         hidden = (token_scale[slot] * jax.nn.silu(shares[:, 0]) * shares[:, 1]).astype(jnp.bfloat16)
-        hidden = lax.all_gather(hidden.reshape(-1, row_count), "group", axis=0, tiled=True)
+        hidden = group_all_gather(hidden.reshape(-1, row_count))
         term = lax.dot_general(
             hidden, weights_out[slot], (((0,), (0,)), ((), ())), preferred_element_type=jnp.float32
         )

time: 598 us -> 462 us (0.77); the launches traced: 596 us -> 454 us
  blocking collectives: 236 us -> 91.8 us
  waiting for transfers between devices: 259 us -> 203 us
  starting transfers between devices: 9.65 us -> 64.1 us
  between operations: 13.2 us -> 0.63 us
  local copies, waits for them, and re-layouts: 40.9 us -> 53.1 us
  other arithmetic: 11.6 us -> 17.8 us
    all_to_all x2 -> x1, blocking collectives: 236 us -> 91.8 us  [on_device(): lax.all_to_all(piece, 'dp', 0, 0, tiled=True).reshape(-1, width_here)]
    all_gather x2 -> x0, waiting for transfers between devices: 144 us -> none  [on_device(): lax.all_gather(hidden.reshape(-1, row_count), 'group', axis=0, tiled=True)]
    ppermute x0 -> x24, waiting for transfers between devices: none -> 130 us  [the longest x2 51.7 us: group_reduce_scatter(): lax.ppermute(other.astype(jnp.bfloat16), 'group', _z_flip(size)).astype(f32)]
    reduce_scatter x2 -> x0, waiting for transfers between devices: 114 us -> none  [on_device(): lax.psum_scatter(partial_here, 'group', scatter_dimension=0, tiled=True)]
    all_to_all x0 -> x1, waiting for transfers between devices: none -> 73.5 us  [on_device(): lax.all_to_all(piece, 'dp', 0, 0, tiled=True).reshape(-1, width_here)]
    ppermute x0 -> x24, starting transfers between devices: none -> 45.1 us  [the longest x2 9.2 us: group_reduce_scatter(): lax.ppermute(other.astype(jnp.bfloat16), 'group', _z_flip(size)).astype(f32)]
    dynamic_slice x0 -> x2, local copies, waits for them, and re-layouts: none -> 6.11 us  [block(): return lax.dynamic_slice_in_dim(x, yy % Y_PARTS * rows, rows, 0)]
  transfers between devices with their start and end apart: 6 -> 27, of which waited for: 4 -> 14; matrix products, arithmetic and copies ran while one was open for 5% -> 8% of each run, Pallas kernels for 0% -> 0%
where the time goes in v2:
time: 462 us; the launch traced here: 454 us
  waiting for transfers between devices  203 us (44%)
  blocking collectives  91.8 us (20%)
  starting transfers between devices  64.1 us (14%)
  local copies, waits for them, and re-layouts  53.1 us (11%)
  matrix products  23 us (5%)
  other arithmetic  17.8 us (4%)
    all_to_all x1, blocking collectives, on_device(): lax.all_to_all(piece, 'dp', 0, 0, tiled=True).reshape(-1, width_here)  91.8 us
    all_to_all x1, waiting for transfers between devices, on_device(): lax.all_to_all(piece, 'dp', 0, 0, tiled=True).reshape(-1, width_here)  73.5 us
    ppermute x2, waiting for transfers between devices, group_reduce_scatter(): lax.ppermute(other.astype(jnp.bfloat16), 'group', _z_flip(size)).astype(f32)  51.7 us
    ppermute x2, waiting for transfers between devices, group_reduce_scatter(): up_far = lax.ppermute(far[:half], 'group', _y_shift(size, 1))  41.3 us
    gather x2, local copies, waits for them, and re-layouts, on_device(): send_in = jnp.take(proj_in, expert_list, axis=0).transpose(0, 1, 3, 2, 4)  27.1 us
    ppermute x2, waiting for transfers between devices, group_reduce_scatter(): relay_up = lax.ppermute(up_far, 'group', _y_shift(size, 1))  15.5 us
    dot_general x2, matrix products, on_device(): jnp.dot(weight_in, tokens.T, preferred_element_type=jnp.float32)  14.5 us
    all_to_all x2, starting transfers between devices, on_device(): weight_out = lax.all_to_all(piece, 'dp', 0, 0, tiled=True)  13.6 us
  transfers between devices with their start and end apart: 27, of which 14 were waited for; matrix products, arithmetic and copies ran while one was open for 8% of the time, Pallas kernels for 0%

profile of v2, /device:TPU:24, one launch (start us, length us, event | category | flops | bytes accessed | tf_op | source)
XLA Modules:
  0.0 453.6 jit_solution(9060701141048886451)
XLA Ops:
  1.7 19.4 %gather_fusion = bf16[64,32,2,896]{3,2,1,0:T(2,128)(2,1)} fusion(bf16[32,32,2,896]{3,2,1,0:T(2,128)(2,1)} %param.7, s32[1024]{0:T(1024)S(1)} %pad_clamp_fusion), kind=kCustom, calls=%fused_computation | custom fusion | bytes 14680320 | tf_op jit(solution)/shard_map/jit(_take)/gather | solution.py:81
  21.1 7.8 %copy.17 = bf16[64,32,2,896]{3,1,2,0:T(8,128)(2,1)} copy(bf16[64,32,2,896]{3,2,1,0:T(2,128)(2,1)} %gather_fusion) | data formatting | bytes 14680064 | tf_op jit(solution)/shard_map/jit(_take)/gather | solution.py:81
  29.0 3.9 select_bitcast_fusion
  32.9 2.6 slice_bitcast_fusion
  35.4 91.8 %all_to_all.20 = bf16[32,2,32,896]{3,2,1,0:T(8,128)(2,1)S(1)} all-to-all(bf16[32,2,32,896]{3,2,1,0:T(8,128)(2,1)S(1)} %get-tuple-element.9), channel_id=1, replica_groups=mesh['dp'=32,'group'=8] {'dp'}, dimensions={0} | all-to-all | bytes 7340032 | tf_op jit(solution)/shard_map/all_to_all | solution.py:89
  127.2 6.3 %convolution_convert_fusion.1 = bf16[2048,1024]{1,0:T(8,128)(2,1)} fusion(bf16[2048,896]{1,0:T(8,128)(2,1)S(1)} %bitcast.76, bf16[1024,896]{1,0:T(8,128)(2,1)S(1)} %copy-done), kind=kOutput, calls=%fused_computation.4 | convolution fusion | flops 3760193536 | bytes 9699328 | tf_op jit(solution)/shard_map/dot_general | solution.py:90
  133.6 5.3 %all-to-all-start.1 = ((bf16[32,2,32,896]{3,2,1,0:T(8,128)(2,1)}), bf16[32,2,32,896]{3,2,1,0:T(8,128)(2,1)}, u32[]{:S(2)}, u32[]{:S(2)}) async-start(bf16[32,2,32,896]{3,2,1,0:T(8,128)(2,1)} %get-tuple-element.10), calls=%async_computation.1 | async-start | bytes 7340032 | tf_op jit(solution)/shard_map/all_to_all | solution.py:89
  138.9 4.2 gather_fusion.1
  143.2 2.5 broadcast_select_fusion
  145.6 2.2 slice_bitcast_fusion.2
  147.9 73.5 %all-to-all-done.1 = bf16[32,2,32,896]{3,2,1,0:T(8,128)(2,1)} async-done(((bf16[32,2,32,896]{3,2,1,0:T(8,128)(2,1)}), bf16[32,2,32,896]{3,2,1,0:T(8,128)(2,1)}, u32[]{:S(2)}, u32[]{:S(2)}) %all-to-all-start.1) | async-done | bytes 3670048 | tf_op jit(solution)/shard_map/all_to_all | solution.py:89
  221.4 8.2 %convolution_convert_fusion = bf16[2048,1024]{1,0:T(8,128)(2,1)} fusion(bf16[2048,896]{1,0:T(8,128)(2,1)} %bitcast.10, bf16[1024,896]{1,0:T(8,128)(2,1)S(1)} %copy-done), kind=kOutput, calls=%fused_computation.3 | convolution fusion | flops 3760193536 | bytes 9699328 | tf_op jit(solution)/shard_map/dot_general | solution.py:90
  229.6 5.9 %all-to-all-start.2 = ((bf16[32,32,896]{2,1,0:T(8,128)(2,1)}), bf16[32,32,896]{2,1,0:T(8,128)(2,1)S(1)}, u32[]{:S(2)}, u32[]{:S(2)}) async-start(bf16[32,32,896]{2,1,0:T(8,128)(2,1)} %get-tuple-element.11), calls=%async_computation.2 | async-start | bytes 3670016 | tf_op jit(solution)/shard_map/all_to_all | solution.py:97
  235.6 3.0 constant_dynamic-slice_fusion.7
  238.9 1.8 collective-permute-start.1
  240.7 2.1 constant_dynamic-slice_fusion.1
  242.8 1.4 collective-permute-start.2
  244.8 30.8 %collective-permute-done.2 = bf16[256,1024]{1,0:T(8,128)(2,1)} collective-permute-done((bf16[256,1024]{1,0:T(8,128)(2,1)S(1)}, bf16[256,1024]{1,0:T(8,128)(2,1)}, u32[]{:S(2)}, u32[]{:S(2)}) %collective-permute-start.2) | collective-permute-done | bytes 524320 | tf_op jit(solution)/shard_map/ppermute | solution.py:36
  275.6 1.5 collective-permute-start.3
  279.1 2.8 collective-permute-start.14
  281.9 3.1 constant_dynamic-slice_fusion.4
  284.9 3.2 collective-permute-start.12
  288.1 2.5 collective-permute-done.3
  291.5 10.5 %collective-permute-done.14 = bf16[256,1024]{1,0:T(8,128)(2,1)} collective-permute-done((bf16[256,1024]{1,0:T(8,128)(2,1)S(1)}, bf16[256,1024]{1,0:T(8,128)(2,1)}, u32[]{:S(2)}, u32[]{:S(2)}) %collective-permute-start.14) | collective-permute-done | bytes 524320 | tf_op jit(solution)/shard_map/ppermute | solution.py:36
  302.0 2.9 collective-permute-start.15
  304.9 2.4 convert_add_fusion.1
  308.7 4.6 %collective-permute-start.6 = (bf16[256,1024]{1,0:T(8,128)(2,1)S(1)}, bf16[256,1024]{1,0:T(8,128)(2,1)S(1)}, u32[]{:S(2)}, u32[]{:S(2)}) collective-permute-start(bf16[256,1024]{1,0:T(8,128)(2,1)S(1)} %dynamic-slice_convert_fusion.1), channel_id=1, source_target_pairs={{0,1},{1,0},{2,3},{3,2},{4,5},{5,4},{6,7},{7,6},{8,9},{9,8},{10,11... | collective-permute-start | bytes 1572872 | tf_op jit(solution)/shard_map/ppermute | solution.py:47
  313.4 7.7 %all-to-all-start.3 = ((bf16[32,32,896]{2,1,0:T(8,128)(2,1)}), bf16[32,32,896]{2,1,0:T(8,128)(2,1)}, u32[]{:S(2)}, u32[]{:S(2)}) async-start(bf16[32,32,896]{2,1,0:T(8,128)(2,1)} %get-tuple-element.12), calls=%async_computation.3 | async-start | bytes 3670016 | tf_op jit(solution)/shard_map/all_to_all | solution.py:97
  321.1 13.0 %collective-permute-done.15 = bf16[256,1024]{1,0:T(8,128)(2,1)} collective-permute-done((bf16[256,1024]{1,0:T(8,128)(2,1)}, bf16[256,1024]{1,0:T(8,128)(2,1)}, u32[]{:S(2)}, u32[]{:S(2)}) %collective-permute-start.15) | collective-permute-done | bytes 524320 | tf_op jit(solution)/shard_map/ppermute | solution.py:38
  334.1 2.7 collective-permute-done.17
  336.8 3.0 convert_add_fusion
  339.9 4.6 %collective-permute-start.18 = (bf16[256,1024]{1,0:T(8,128)(2,1)S(1)}, bf16[256,1024]{1,0:T(8,128)(2,1)S(1)}, u32[]{:S(2)}, u32[]{:S(2)}) collective-permute-start(bf16[256,1024]{1,0:T(8,128)(2,1)S(1)} %dynamic-slice_convert_fusion), channel_id=1, source_target_pairs={{0,1},{1,0},{2,3},{3,2},{4,5},{5,4},{6,7},{7,6},{8,9},{9,8},{10,11... | collective-permute-start | bytes 1572872 | tf_op jit(solution)/shard_map/ppermute | solution.py:47
  345.0 1.5 collective-permute-start.7
  346.5 51.7 %collective-permute-done.18 = bf16[256,1024]{1,0:T(8,128)(2,1)S(1)} collective-permute-done((bf16[256,1024]{1,0:T(8,128)(2,1)S(1)}, bf16[256,1024]{1,0:T(8,128)(2,1)S(1)}, u32[]{:S(2)}, u32[]{:S(2)}) %collective-permute-start.18) | collective-permute-done | bytes 524320 | tf_op jit(solution)/shard_map/ppermute | solution.py:47
  398.6 4.8 %collective-permute-start.19 = (bf16[128,1024]{1,0:T(8,128)(2,1)S(1)}, bf16[128,1024]{1,0:T(8,128)(2,1)S(1)}, u32[]{:S(2)}, u32[]{:S(2)}) collective-permute-start(bf16[128,1024]{1,0:T(8,128)(2,1)S(1)} %fusion), channel_id=1, source_target_pairs={{0,1},{1,0},{2,3},{3,2},{4,5},{5,4},{6,7},{7,6},{8,9},{9,8},{10,11... | collective-permute-start | bytes 786440 | tf_op jit(solution)/shard_map/ppermute | solution.py:55
  404.0 3.0 collective-permute-start.8
  407.0 3.5 collective-permute-done.19
  410.5 1.6 broadcast.27.clone
  413.2 2.9 collective-permute-start.20
  416.1 3.3 collective-permute-done.8
  419.4 3.8 collective-permute-start.10
  425.0 5.6 %collective-permute-done.20 = bf16[256,1024]{1,0:T(8,128)(2,1)S(1)} collective-permute-done((bf16[256,1024]{1,0:T(8,128)(2,1)S(1)}, bf16[256,1024]{1,0:T(8,128)(2,1)S(1)}, u32[]{:S(2)}, u32[]{:S(2)}) %collective-permute-start.20) | collective-permute-done | bytes 524320 | tf_op jit(solution)/shard_map/ppermute | solution.py:57
  430.6 4.0 collective-permute-start.22
  434.7 1.5 collective-permute-done.10
  436.2 3.8 collective-permute-done.11
  440.1 1.8 maximum_dynamic-update-slice_fusion
  444.9 4.7 %fusion.13 = f32[1024,896]{1,0:T(8,128)S(1)} fusion(bf16[1024,1024]{1,0:T(8,128)(2,1)} %maximum_dynamic-update-slice_fusion.1, bf16[1024,896]{1,0:T(8,128)(2,1)} %bitcast.19), kind=kOutput, calls=%fused_computation.60 | convolution fusion | flops 1879048192 | bytes 7602176 | tf_op jit(solution)/shard_map/dot_general | solution.py:106
  449.6 3.8 add_convert_fusion
  (76 shorter events, 14.4 us)
Async XLA Ops:
  0.0 127.2 %copy-start = (bf16[1024,896]{1,0:T(8,128)(2,1)S(1)}, bf16[1024,896]{1,0:T(8,128)(2,1)}, u32[]{:S(2)}) copy-start(bf16[1024,896]{1,0:T(8,128)(2,1)} %param.6) | copy-start | bytes 5505028
  133.6 87.9 %all-to-all-start.1 = ((bf16[32,2,32,896]{3,2,1,0:T(8,128)(2,1)}), bf16[32,2,32,896]{3,2,1,0:T(8,128)(2,1)}, u32[]{:S(2)}, u32[]{:S(2)}) async-start(bf16[32,2,32,896]{3,2,1,0:T(8,128)(2,1)} %get-tuple-element.10), calls=%async_computation.1 | async-start | bytes 7340032 | tf_op jit(solution)/shard_map/all_to_all | solution.py:89
  229.6 83.7 %all-to-all-start.2 = ((bf16[32,32,896]{2,1,0:T(8,128)(2,1)}), bf16[32,32,896]{2,1,0:T(8,128)(2,1)S(1)}, u32[]{:S(2)}, u32[]{:S(2)}) async-start(bf16[32,32,896]{2,1,0:T(8,128)(2,1)} %get-tuple-element.11), calls=%async_computation.2 | async-start | bytes 3670016 | tf_op jit(solution)/shard_map/all_to_all | solution.py:97
  238.7 38.4 %copy-start.9 = (s32[32,2,8]{0,2,1:T(8,128)S(1)}, s32[32,2,8]{0,2,1:T(8,128)}, u32[]{:S(2)}) copy-start(s32[32,2,8]{0,2,1:T(8,128)} %param.10) | copy-start | bytes 6148
  238.7 43.2 %collective-permute-start = (bf16[512,1024]{1,0:T(8,128)(2,1)}, bf16[512,1024]{1,0:T(8,128)(2,1)S(1)}, u32[]{:S(2)}, u32[]{:S(2)}) collective-permute-start(bf16[512,1024]{1,0:T(8,128)(2,1)} %get-tuple-element.21), channel_id=1, source_target_pairs={{0,2},{1,3},{2,4},{3,5},{4,6},{5,7},{6,0},{7,1},{8,10},{9,11},{10,... | collective-permute-start | bytes 3145736 | tf_op jit(solution)/shard_map/ppermute | solution.py:34
  238.9 46.0 %collective-permute-start.1 = (bf16[512,1024]{1,0:T(8,128)(2,1)}, bf16[512,1024]{1,0:T(8,128)(2,1)}, u32[]{:S(2)}, u32[]{:S(2)}) collective-permute-start(bf16[512,1024]{1,0:T(8,128)(2,1)} %get-tuple-element.22), channel_id=1, source_target_pairs={{0,6},{1,7},{2,0},{3,1},{4,2},{5,3},{6,4},{7,5},{8,14},{9,15},{10,... | collective-permute-start | bytes 3145736 | tf_op jit(solution)/shard_map/ppermute | solution.py:35
  242.8 32.8 %collective-permute-start.2 = (bf16[256,1024]{1,0:T(8,128)(2,1)S(1)}, bf16[256,1024]{1,0:T(8,128)(2,1)}, u32[]{:S(2)}, u32[]{:S(2)}) collective-permute-start(bf16[256,1024]{1,0:T(8,128)(2,1)S(1)} %get-tuple-element.19), channel_id=1, source_target_pairs={{0,2},{1,3},{2,4},{3,5},{4,6},{5,7},{6,0},{7,1},{8,10},{9,11},{10,... | collective-permute-start | bytes 1572872 | tf_op jit(solution)/shard_map/ppermute | solution.py:36
  244.2 33.0 %collective-permute-start.4 = (bf16[256,1024]{1,0:T(8,128)(2,1)}, bf16[256,1024]{1,0:T(8,128)(2,1)}, u32[]{:S(2)}, u32[]{:S(2)}) collective-permute-start(bf16[256,1024]{1,0:T(8,128)(2,1)} %get-tuple-element.20), channel_id=1, source_target_pairs={{0,6},{1,7},{2,0},{3,1},{4,2},{5,3},{6,4},{7,5},{8,14},{9,15},{10,... | collective-permute-start | bytes 1572872 | tf_op jit(solution)/shard_map/ppermute | solution.py:37
  275.6 15.1 %collective-permute-start.3 = (bf16[256,1024]{1,0:T(8,128)(2,1)}, bf16[256,1024]{1,0:T(8,128)(2,1)S(1)}, u32[]{:S(2)}, u32[]{:S(2)}) collective-permute-start(bf16[256,1024]{1,0:T(8,128)(2,1)} %collective-permute-done.2), channel_id=1, source_target_pairs={{0,2},{1,3},{2,4},{3,5},{4,6},{5,7},{6,0},{7,1},{8,10},{9,11},{10,... | collective-permute-start | bytes 1572872 | tf_op jit(solution)/shard_map/ppermute | solution.py:38
  277.2 27.6 %collective-permute-start.5 = (bf16[256,1024]{1,0:T(8,128)(2,1)}, bf16[256,1024]{1,0:T(8,128)(2,1)S(1)}, u32[]{:S(2)}, u32[]{:S(2)}) collective-permute-start(bf16[256,1024]{1,0:T(8,128)(2,1)} %collective-permute-done.4), channel_id=1, source_target_pairs={{0,6},{1,7},{2,0},{3,1},{4,2},{5,3},{6,4},{7,5},{8,14},{9,15},{10,... | collective-permute-start | bytes 1572872 | tf_op jit(solution)/shard_map/ppermute | solution.py:39
  279.1 22.9 %collective-permute-start.14 = (bf16[256,1024]{1,0:T(8,128)(2,1)S(1)}, bf16[256,1024]{1,0:T(8,128)(2,1)}, u32[]{:S(2)}, u32[]{:S(2)}) collective-permute-start(bf16[256,1024]{1,0:T(8,128)(2,1)S(1)} %get-tuple-element.23), channel_id=1, source_target_pairs={{0,2},{1,3},{2,4},{3,5},{4,6},{5,7},{6,0},{7,1},{8,10},{9,11},{10,... | collective-permute-start | bytes 1572872 | tf_op jit(solution)/shard_map/ppermute | solution.py:36
  281.8 9.6 %copy-start.8 = (f32[1024,2]{0,1:T(2,128)S(1)}, f32[1024,2]{0,1:T(2,128)}, u32[]{:S(2)}) copy-start(f32[1024,2]{0,1:T(2,128)} %param.11) | copy-start | bytes 24580
  281.8 23.0 %collective-permute-start.16 = (bf16[256,1024]{1,0:T(8,128)(2,1)S(1)}, bf16[256,1024]{1,0:T(8,128)(2,1)}, u32[]{:S(2)}, u32[]{:S(2)}) collective-permute-start(bf16[256,1024]{1,0:T(8,128)(2,1)S(1)} %get-tuple-element.24), channel_id=1, source_target_pairs={{0,6},{1,7},{2,0},{3,1},{4,2},{5,3},{6,4},{7,5},{8,14},{9,15},{10,... | collective-permute-start | bytes 1572872 | tf_op jit(solution)/shard_map/ppermute | solution.py:37
  284.9 51.9 %collective-permute-start.12 = (bf16[512,1024]{1,0:T(8,128)(2,1)}, bf16[512,1024]{1,0:T(8,128)(2,1)}, u32[]{:S(2)}, u32[]{:S(2)}) collective-permute-start(bf16[512,1024]{1,0:T(8,128)(2,1)} %get-tuple-element.25), channel_id=1, source_target_pairs={{0,2},{1,3},{2,4},{3,5},{4,6},{5,7},{6,0},{7,1},{8,10},{9,11},{10,... | collective-permute-start | bytes 3145736 | tf_op jit(solution)/shard_map/ppermute | solution.py:34
  290.6 46.2 %collective-permute-start.13 = (bf16[512,1024]{1,0:T(8,128)(2,1)}, bf16[512,1024]{1,0:T(8,128)(2,1)}, u32[]{:S(2)}, u32[]{:S(2)}) collective-permute-start(bf16[512,1024]{1,0:T(8,128)(2,1)} %get-tuple-element.26), channel_id=1, source_target_pairs={{0,6},{1,7},{2,0},{3,1},{4,2},{5,3},{6,4},{7,5},{8,14},{9,15},{10,... | collective-permute-start | bytes 3145736 | tf_op jit(solution)/shard_map/ppermute | solution.py:35
  302.0 32.1 %collective-permute-start.15 = (bf16[256,1024]{1,0:T(8,128)(2,1)}, bf16[256,1024]{1,0:T(8,128)(2,1)}, u32[]{:S(2)}, u32[]{:S(2)}) collective-permute-start(bf16[256,1024]{1,0:T(8,128)(2,1)} %collective-permute-done.14), channel_id=1, source_target_pairs={{0,2},{1,3},{2,4},{3,5},{4,6},{5,7},{6,0},{7,1},{8,10},{9,11},{10,... | collective-permute-start | bytes 1572872 | tf_op jit(solution)/shard_map/ppermute | solution.py:38
  304.9 31.9 %collective-permute-start.17 = (bf16[256,1024]{1,0:T(8,128)(2,1)}, bf16[256,1024]{1,0:T(8,128)(2,1)}, u32[]{:S(2)}, u32[]{:S(2)}) collective-permute-start(bf16[256,1024]{1,0:T(8,128)(2,1)} %collective-permute-done.16), channel_id=1, source_target_pairs={{0,6},{1,7},{2,0},{3,1},{4,2},{5,3},{6,4},{7,5},{8,14},{9,15},{10,... | collective-permute-start | bytes 1572872 | tf_op jit(solution)/shard_map/ppermute | solution.py:39
  307.3 1.4 copy-start.2
  308.7 35.8 %collective-permute-start.6 = (bf16[256,1024]{1,0:T(8,128)(2,1)S(1)}, bf16[256,1024]{1,0:T(8,128)(2,1)S(1)}, u32[]{:S(2)}, u32[]{:S(2)}) collective-permute-start(bf16[256,1024]{1,0:T(8,128)(2,1)S(1)} %dynamic-slice_convert_fusion.1), channel_id=1, source_target_pairs={{0,1},{1,0},{2,3},{3,2},{4,5},{5,4},{6,7},{7,6},{8,9},{9,8},{10,11... | collective-permute-start | bytes 1572872 | tf_op jit(solution)/shard_map/ppermute | solution.py:47
  313.4 26.5 %copy-start.6 = (bf16[32,32,896]{2,1,0:T(8,128)(2,1)}, bf16[32,32,896]{2,1,0:T(8,128)(2,1)S(1)}, u32[]{:S(2)}) copy-start(bf16[32,32,896]{2,1,0:T(8,128)(2,1)S(1)} %all-to-all-done.2) | copy-start | bytes 5505028
  313.4 131.6 %all-to-all-start.3 = ((bf16[32,32,896]{2,1,0:T(8,128)(2,1)}), bf16[32,32,896]{2,1,0:T(8,128)(2,1)}, u32[]{:S(2)}, u32[]{:S(2)}) async-start(bf16[32,32,896]{2,1,0:T(8,128)(2,1)} %get-tuple-element.12), calls=%async_computation.3 | async-start | bytes 3670016 | tf_op jit(solution)/shard_map/all_to_all | solution.py:97
  321.1 23.4 %copy-start.3 = (f32[512,1024]{1,0:T(8,128)S(1)}, f32[512,1024]{1,0:T(8,128)}, u32[]{:S(2)}) copy-start(f32[512,1024]{1,0:T(8,128)} %copy-done.2) | copy-start | bytes 6291460
  339.9 58.2 %collective-permute-start.18 = (bf16[256,1024]{1,0:T(8,128)(2,1)S(1)}, bf16[256,1024]{1,0:T(8,128)(2,1)S(1)}, u32[]{:S(2)}, u32[]{:S(2)}) collective-permute-start(bf16[256,1024]{1,0:T(8,128)(2,1)S(1)} %dynamic-slice_convert_fusion), channel_id=1, source_target_pairs={{0,1},{1,0},{2,3},{3,2},{4,5},{5,4},{6,7},{7,6},{8,9},{9,8},{10,11... | collective-permute-start | bytes 1572872 | tf_op jit(solution)/shard_map/ppermute | solution.py:47
  345.0 58.6 %collective-permute-start.7 = (bf16[128,1024]{1,0:T(8,128)(2,1)S(1)}, bf16[128,1024]{1,0:T(8,128)(2,1)S(1)}, u32[]{:S(2)}, u32[]{:S(2)}) collective-permute-start(bf16[128,1024]{1,0:T(8,128)(2,1)S(1)} %fusion.5), channel_id=1, source_target_pairs={{0,1},{1,0},{2,3},{3,2},{4,5},{5,4},{6,7},{7,6},{8,9},{9,8},{10,11... | collective-permute-start | bytes 786440 | tf_op jit(solution)/shard_map/ppermute | solution.py:55
  398.6 12.0 %collective-permute-start.19 = (bf16[128,1024]{1,0:T(8,128)(2,1)S(1)}, bf16[128,1024]{1,0:T(8,128)(2,1)S(1)}, u32[]{:S(2)}, u32[]{:S(2)}) collective-permute-start(bf16[128,1024]{1,0:T(8,128)(2,1)S(1)} %fusion), channel_id=1, source_target_pairs={{0,1},{1,0},{2,3},{3,2},{4,5},{5,4},{6,7},{7,6},{8,9},{9,8},{10,11... | collective-permute-start | bytes 786440 | tf_op jit(solution)/shard_map/ppermute | solution.py:55
  404.0 15.4 %copy-start.4 = (bf16[1024,1024]{1,0:T(8,128)(2,1)}, bf16[1024,1024]{1,0:T(8,128)(2,1)S(1)}, u32[]{:S(2)}) copy-start(bf16[1024,1024]{1,0:T(8,128)(2,1)S(1)} %get-tuple-element.13) | copy-start | bytes 6291460
  404.0 15.3 %collective-permute-start.8 = (bf16[256,1024]{1,0:T(8,128)(2,1)S(1)}, bf16[256,1024]{1,0:T(8,128)(2,1)S(1)}, u32[]{:S(2)}, u32[]{:S(2)}) collective-permute-start(bf16[256,1024]{1,0:T(8,128)(2,1)S(1)} %get-tuple-element.14), channel_id=1, source_target_pairs={{0,2},{1,3},{2,4},{3,5},{4,6},{5,7},{6,0},{7,1},{8,10},{9,11},{10,... | collective-permute-start | bytes 1572872 | tf_op jit(solution)/shard_map/ppermute | solution.py:57
  407.0 16.1 %collective-permute-start.9 = (bf16[256,1024]{1,0:T(8,128)(2,1)S(1)}, bf16[256,1024]{1,0:T(8,128)(2,1)S(1)}, u32[]{:S(2)}, u32[]{:S(2)}) collective-permute-start(bf16[256,1024]{1,0:T(8,128)(2,1)S(1)} %get-tuple-element.14), channel_id=1, source_target_pairs={{0,6},{1,7},{2,0},{3,1},{4,2},{5,3},{6,4},{7,5},{8,14},{9,15},{10,... | collective-permute-start | bytes 1572872 | tf_op jit(solution)/shard_map/ppermute | solution.py:58
  413.2 17.4 %collective-permute-start.20 = (bf16[256,1024]{1,0:T(8,128)(2,1)S(1)}, bf16[256,1024]{1,0:T(8,128)(2,1)S(1)}, u32[]{:S(2)}, u32[]{:S(2)}) collective-permute-start(bf16[256,1024]{1,0:T(8,128)(2,1)S(1)} %get-tuple-element.16), channel_id=1, source_target_pairs={{0,2},{1,3},{2,4},{3,5},{4,6},{5,7},{6,0},{7,1},{8,10},{9,11},{10,... | collective-permute-start | bytes 1572872 | tf_op jit(solution)/shard_map/ppermute | solution.py:57
  416.1 18.6 %collective-permute-start.21 = (bf16[256,1024]{1,0:T(8,128)(2,1)S(1)}, bf16[256,1024]{1,0:T(8,128)(2,1)S(1)}, u32[]{:S(2)}, u32[]{:S(2)}) collective-permute-start(bf16[256,1024]{1,0:T(8,128)(2,1)S(1)} %get-tuple-element.16), channel_id=1, source_target_pairs={{0,6},{1,7},{2,0},{3,1},{4,2},{5,3},{6,4},{7,5},{8,14},{9,15},{10,... | collective-permute-start | bytes 1572872 | tf_op jit(solution)/shard_map/ppermute | solution.py:58
  419.4 16.8 %collective-permute-start.10 = (bf16[128,1024]{1,0:T(8,128)(2,1)S(1)}, bf16[128,1024]{1,0:T(8,128)(2,1)S(1)}, u32[]{:S(2)}, u32[]{:S(2)}) collective-permute-start(bf16[128,1024]{1,0:T(8,128)(2,1)S(1)} %slice.80), channel_id=1, source_target_pairs={{0,2},{1,3},{2,4},{3,5},{4,6},{5,7},{6,0},{7,1},{8,10},{9,11},{10,... | collective-permute-start | bytes 786440 | tf_op jit(solution)/shard_map/ppermute | solution.py:59
  423.2 16.9 %collective-permute-start.11 = (bf16[128,1024]{1,0:T(8,128)(2,1)S(1)}, bf16[128,1024]{1,0:T(8,128)(2,1)}, u32[]{:S(2)}, u32[]{:S(2)}) collective-permute-start(bf16[128,1024]{1,0:T(8,128)(2,1)S(1)} %slice.81), channel_id=1, source_target_pairs={{0,6},{1,7},{2,0},{3,1},{4,2},{5,3},{6,4},{7,5},{8,14},{9,15},{10,... | collective-permute-start | bytes 786440 | tf_op jit(solution)/shard_map/ppermute | solution.py:60
  430.6 12.9 %collective-permute-start.22 = (bf16[128,1024]{1,0:T(8,128)(2,1)S(1)}, bf16[128,1024]{1,0:T(8,128)(2,1)S(1)}, u32[]{:S(2)}, u32[]{:S(2)}) collective-permute-start(bf16[128,1024]{1,0:T(8,128)(2,1)S(1)} %slice.87), channel_id=1, source_target_pairs={{0,2},{1,3},{2,4},{3,5},{4,6},{5,7},{6,0},{7,1},{8,10},{9,11},{10,... | collective-permute-start | bytes 786440 | tf_op jit(solution)/shard_map/ppermute | solution.py:59
  434.6 9.4 %collective-permute-start.23 = (bf16[128,1024]{1,0:T(8,128)(2,1)S(1)}, bf16[128,1024]{1,0:T(8,128)(2,1)S(1)}, u32[]{:S(2)}, u32[]{:S(2)}) collective-permute-start(bf16[128,1024]{1,0:T(8,128)(2,1)S(1)} %slice.88), channel_id=1, source_target_pairs={{0,6},{1,7},{2,0},{3,1},{4,2},{5,3},{6,4},{7,5},{8,14},{9,15},{10,... | collective-permute-start | bytes 786440 | tf_op jit(solution)/shard_map/ppermute | solution.py:60
  444.9 4.7 %copy-start.5 = (bf16[1024,1024]{1,0:T(8,128)(2,1)S(1)}, bf16[1024,1024]{1,0:T(8,128)(2,1)}, u32[]{:S(2)}) copy-start(bf16[1024,1024]{1,0:T(8,128)(2,1)} %maximum_dynamic-update-slice_fusion) | copy-start | bytes 6291460
  444.9 4.7 %copy-start.7 = (bf16[32,32,896]{2,1,0:T(8,128)(2,1)S(1)}, bf16[32,32,896]{2,1,0:T(8,128)(2,1)}, u32[]{:S(2)}) copy-start(bf16[32,32,896]{2,1,0:T(8,128)(2,1)} %copy-done.6) | copy-start | bytes 5505028
  449.6 3.8 copy-start.1
